TPU v7x, 128 devices: a whole 4x4x4 slice. The times are simulated.
128 devices in a mesh: dp: 4 (over y), row: 4 (over z_hi, core), col: 8 (over x, z_lo).
Axes of the slice: x: 4, y: 4, z: 4 (z_hi: 2, z_lo: 2; z = z_hi * 2 + z_lo), core: 2. Of those that a mesh axis runs over, the one named last changes fastest.
Arguments:
- latent: bfloat16 [4, 64, 64, 2240], P('dp', 'row', 'col'), may hold values from -40 to 40
- query_weight: bfloat16 [2240, 1120], replicated, may hold values from -0.125 to 0.125
- key_weight: bfloat16 [2240, 1120], replicated, may hold values from -0.125 to 0.125
- value_weight: bfloat16 [2240, 1120], replicated, may hold values from -0.125 to 0.125
- upstream_grad: bfloat16 [4, 64, 64, 1120], P('dp', 'row', 'col'), may hold values from -6 to 6
Outputs:
- latent_grad: bfloat16 [4, 64, 64, 2240], P('dp', 'row', 'col')
- query_weight_grad: float32 [2240, 1120], P(('row', 'col'), 'dp')
- key_weight_grad: float32 [2240, 1120], P(('row', 'col'), 'dp')
- value_weight_grad: float32 [2240, 1120], P(('row', 'col'), 'dp')
All inputs are finite; a program needn't handle non-finite values.
Results may differ from a plain program's by a relative error of at most 0.039.
Values sent between devices are 32-bit elements; how exact they have to be, the bound alone decides.
No kernel may reach another device: no remote copies, remote signals or barrier semaphores. Data moves between devices by JAX's collectives and lax.ppermute only.
A program may use at most 192 MiB of HBM per device.

v0:
```python
import math
import jax
import jax.numpy as jnp
from jax import lax
from jax.sharding import PartitionSpec as P

D = 2240
HD = 112
HEADS = 10
EPSILON = 1e-15
HIGHEST_PRECISION = lax.Precision.HIGHEST


def project(token_rows, weight):
    return jnp.dot(token_rows, weight, preferred_element_type=jnp.float32).astype(jnp.bfloat16)


def back_project(gradient, weight):
    return lax.dot_general(
        gradient, weight, (((1,), (1,)), ((), ())), preferred_element_type=jnp.float32
    )


def body(latent, query_weight, key_weight, value_weight, upstream_grad):
    grid_devices = lax.axis_size("row") * lax.axis_size("col")
    replicas = lax.axis_size("dp")
    token_rows = latent.reshape(-1, D)
    local_count = token_rows.shape[0]
    image_tokens = local_count * grid_devices
    loss_scale = 4.0 * math.sqrt(image_tokens)
    normalizer = 1.0 / math.sqrt(image_tokens * replicas)
    head_width = HEADS * HD
    key_rows = project(token_rows, key_weight)
    value_rows = project(token_rows, value_weight)
    relu_key = jax.nn.relu(key_rows).reshape(-1, HEADS, HD)
    value_heads = value_rows.reshape(-1, HEADS, HD)
    local_state = jnp.einsum(
        "thj,thm->hjm", relu_key, value_heads, preferred_element_type=jnp.float32
    )
    local_total = jnp.sum(relu_key, axis=0, dtype=jnp.float32)
    key_state, key_total = lax.psum((local_state, local_total), ("row", "col"))
    query_rows = project(token_rows, query_weight)
    query_heads = query_rows.reshape(-1, HEADS, HD)
    relu_query = jax.nn.relu(query_heads)
    denominator = (
        jnp.einsum(
            "thj,hj->th",
            relu_query,
            key_total,
            precision=HIGHEST_PRECISION,
            preferred_element_type=jnp.float32,
        )
        + EPSILON
    )
    attended = (
        jnp.einsum(
            "thj,hjm->thm",
            relu_query,
            key_state,
            precision=HIGHEST_PRECISION,
            preferred_element_type=jnp.float32,
        )
        / denominator[:, :, None]
    )
    cotangent = upstream_grad.reshape(-1, HEADS, HD).astype(jnp.float32) * loss_scale
    grad_numer = cotangent / denominator[:, :, None]
    grad_denom = -jnp.sum(cotangent * attended, axis=2) / denominator
    grad_numer_low = grad_numer.astype(jnp.bfloat16)
    local_state_grad = jnp.einsum(
        "thj,thm->hjm", relu_query, grad_numer_low, preferred_element_type=jnp.float32
    )
    local_total_grad = jnp.einsum(
        "thj,th->hj",
        relu_query,
        grad_denom,
        precision=HIGHEST_PRECISION,
        preferred_element_type=jnp.float32,
    )
    state_grad, total_grad = lax.psum((local_state_grad, local_total_grad), ("row", "col"))
    grad_relu_query = (
        jnp.einsum(
            "thm,hjm->thj",
            grad_numer_low,
            key_state,
            precision=HIGHEST_PRECISION,
            preferred_element_type=jnp.float32,
        )
        + grad_denom[:, :, None] * key_total[None]
    )
    grad_query = (
        jnp.where(query_heads > 0, grad_relu_query, 0.0)
        .reshape(-1, head_width)
        .astype(jnp.bfloat16)
    )
    grad_value = (
        jnp.einsum(
            "thj,hjm->thm",
            relu_key,
            state_grad,
            precision=HIGHEST_PRECISION,
            preferred_element_type=jnp.float32,
        )
        .reshape(-1, head_width)
        .astype(jnp.bfloat16)
    )
    grad_relu_key = (
        jnp.einsum(
            "thm,hjm->thj",
            value_heads,
            state_grad,
            precision=HIGHEST_PRECISION,
            preferred_element_type=jnp.float32,
        )
        + total_grad[None]
    )
    grad_key = (
        jnp.where(key_rows.reshape(-1, HEADS, HD) > 0, grad_relu_key, 0.0)
        .reshape(-1, head_width)
        .astype(jnp.bfloat16)
    )
    summed = back_project(grad_query, query_weight) + back_project(grad_key, key_weight)
    summed = summed + back_project(grad_value, value_weight)
    latent_grad = summed.astype(jnp.bfloat16).reshape(latent.shape)
    stacked = jnp.stack([grad_query, grad_key, grad_value], axis=1).reshape(
        local_count, 3, replicas, head_width // replicas
    )
    stacked = jnp.transpose(stacked, (0, 2, 1, 3)).reshape(local_count, 3 * head_width)
    row_block = lax.psum_scatter(
        lax.dot_general(
            token_rows, stacked, (((0,), (0,)), ((), ())), preferred_element_type=jnp.float32
        )
        * normalizer,
        ("row", "col"),
        scatter_dimension=0,
        tiled=True,
    )
    weight_block = lax.psum_scatter(row_block, "dp", scatter_dimension=1, tiled=True)
    weight_block = weight_block.reshape(weight_block.shape[0], 3, head_width // replicas)
    return (latent_grad, weight_block[:, 0], weight_block[:, 1], weight_block[:, 2])


def solution(mesh):
    return jax.shard_map(
        body,
        mesh=mesh,
        in_specs=(P("dp", "row", "col", None), P(), P(), P(), P("dp", "row", "col", None)),
        out_specs=(
            P("dp", "row", "col", None),
            P(("row", "col"), "dp"),
            P(("row", "col"), "dp"),
            P(("row", "col"), "dp"),
        ),
        check_vma=False,
    )
```

profile of v0, /device:TPU:1, one launch (start us, length us, event | category | flops | bytes accessed | tf_op | source)
XLA Modules:
  0.0 548.4 jit_solution(5383486594765757244)
XLA Ops:
  7.2 1.0 copy-done
  8.2 4.7 broadcast_compare_fusion.1
  13.0 4.6 broadcast_maximum_fusion.1
  17.6 2.2 convolution_convert_fusion
  21.1 62.9 %psum.29 = f32[10,112]{1,0:T(8,128)S(1)} all-reduce(f32[10,112]{1,0:T(8,128)S(1)} %reduce_sum.21), channel_id=1, replica_groups=mesh['dp'=4,'row'=4,'col'=8] {'row','col'}, use_global_device_ids=true, to_apply=%region_2.3 | all-reduce | flops 1120 | bytes 8960 | tf_op jit(solution)/shard_map/psum | solution.py:41
  84.4 1.1 fusion.21
  85.5 1.2 fusion.19
  86.8 109.0 %all-reduce.8.cloned.1.call-done = (f32[10,112,112]{2,1,0:T(8,128)}, f32[10,112,112]{2,1,0:T(8,128)}) async-done(((f32[10,112,112]{2,1,0:T(8,128)}, f32[10,112,112]{2,1,0:T(8,128)}), (f32[10,112,112]{2,1,0:T(8,128)}, f32[10,112,112]{2,1,0:T(8,128)})) %all-reduce.8.cloned.1.call-update) | async-done | bytes 1003536 | tf_op jit(solution)/shard_map/psum | solution.py:41
  195.8 1.8 fusion.9
  197.6 1.6 fusion.8
  199.7 59.9 %psum.31 = f32[10,112]{1,0:T(8,128)S(1)} all-reduce(f32[10,112]{1,0:T(8,128)S(1)} %bitcast.132), channel_id=1, replica_groups=mesh['dp'=4,'row'=4,'col'=8] {'row','col'}, use_global_device_ids=true, to_apply=%region_5.6 | all-reduce | flops 1120 | bytes 8960 | tf_op jit(solution)/shard_map/psum | solution.py:79
  259.7 0.6 convolution_convert_fusion.3
  260.9 12.2 %multiply_bitcast_fusion = f32[2240,3360]{0,1:T(8,128)} fusion(bf16[128,3360]{0,1:T(8,128)(2,1)S(1)} %bitcast.110, bf16[1,16,8,2240]{3,2,1,0:T(8,128)(2,1)S(1)} %copy-done), kind=kOutput, calls=%fused_computation | convolution fusion | flops 1934284800 | bytes 31539200 | tf_op jit(solution)/shard_map/dot_general | solution.py:129
  275.0 232.8 %all-reduce.6.cloned.1.call-done = f32[2240,3360]{0,1:T(8,128)} async-done(((f32[2240,3360]{0,1:T(8,128)}), f32[2240,3360]{0,1:T(8,128)}) %all-reduce.6.cloned.1.call-update) | async-done | bytes 30105616
  507.8 3.7 constant_dynamic-slice_fusion
  511.5 4.1 fusion.22
  515.7 4.1 convolution_add_fusion.1
  519.9 1.6 fusion
  521.4 1.1 copy.31
  522.5 16.0 %reduce-scatter.5.cloned.1.call-done = f32[70,840]{0,1:T(8,128)} async-done(((f32[70,3360]{0,1:T(8,128)}), f32[70,840]{0,1:T(8,128)}) %reduce-scatter.5.cloned.1.call-update) | async-done | bytes 235216
  538.5 1.1 fusion.20
  539.5 0.8 copy.46
  540.3 0.8 copy.47
  541.1 0.8 copy.48
  (37 shorter events, 4.1 us)
Async XLA Ops:
  7.2 1.1 copy-start
  7.2 188.6 %all-reduce.8.cloned.1.call-start = ((), (), s32[]{:S(2)}) async-start(), calls=%async_computation.3 | async-start | bytes 2293760 | tf_op jit(solution)/shard_map/psum | solution.py:41
  8.2 9.4 %copy-start.2 = (bf16[2240,1120]{1,0:T(8,128)(2,1)S(1)}, bf16[2240,1120]{1,0:T(8,128)(2,1)}, u32[]{:S(2)}) copy-start(bf16[2240,1120]{1,0:T(8,128)(2,1)} %param.8) | copy-start | bytes 15052804
  13.0 6.9 %copy-start.4 = (bf16[1,16,8,1120]{3,2,1,0:T(8,128)(2,1)S(1)}, bf16[1,16,8,1120]{3,2,1,0:T(8,128)(2,1)}, u32[]{:S(2)}) copy-start(bf16[1,16,8,1120]{3,2,1,0:T(8,128)(2,1)} %param.9) | copy-start | bytes 860164
  86.7 421.1 %all-reduce.6.cloned.1.call-start = ((), (), s32[]{:S(2)}) async-start(), calls=%async_computation.1 | async-start | bytes 61931520
  195.8 63.8 %copy-start.3 = (f32[10,112,112]{2,1,0:T(8,128)S(1)}, f32[10,112,112]{2,1,0:T(8,128)}, u32[]{:S(2)}) copy-start(f32[10,112,112]{2,1,0:T(8,128)} %get-tuple-element.9) | copy-start | bytes 1505284
  273.1 0.7 copy-start.5
  273.1 265.3 %reduce-scatter.5.cloned.1.call-start = ((), (), s32[]{:S(2)}) async-start(), calls=%async_computation.2 | async-start | bytes 2150400
  511.5 8.3 %slice-start = ((s8[5160960]{0:T(1024)(128)(4,1)}), s8[4194304]{0:T(1024)(128)(4,1)S(1)}, s32[]{:S(2)}) async-start(s8[5160960]{0:T(1024)(128)(4,1)} %bitcast.108), calls=%async_computation.4 | async-start | bytes 8388608
  515.7 4.2 slice-start.1
  519.8 22.0 %copy-start.1 = (bf16[1,16,8,2240]{3,2,1,0:T(8,128)(2,1)S(1)}, bf16[1,16,8,2240]{3,2,1,0:T(8,128)(2,1)}, u32[]{:S(2)}) copy-start(bf16[1,16,8,2240]{3,2,1,0:T(8,128)(2,1)} %param.5) | copy-start | bytes 1720324
Sparse Core Ops, SparseCore 0:
  86.8 108.9 all-reduce.7
  273.2 234.5 all-reduce.5
  511.6 26.7 reduce-scatter.4
where the time goes:
time: 549 us; the launch traced here: 548 us
  waiting for transfers between devices  358 us (65%)
  blocking collectives  123 us (22%)
  matrix products  41.2 us (8%)
  between operations  14.6 us (3%)
  local copies, waits for them, and re-layouts  11.3 us (2%)
    unnamed x5, waiting for transfers between devices  249 us
    psum x1, waiting for transfers between devices, body(): key_state, key_total = lax.psum((local_state, local_total), ('row', 'col'))  109 us
    psum x1, blocking collectives, body(): key_state, key_total = lax.psum((local_state, local_total), ('row', 'col'))  62.9 us
    psum x1, blocking collectives, body(): lax.psum((local_state_grad, local_total_grad), ('row', 'col'))  59.9 us
    dot_general x1, matrix products, body(): lax.dot_general(token_rows, stacked, (((0,), (0,)), ((), ())), preferred_...  12.2 us
    dot_general x3, matrix products, project(): jnp.dot(token_rows, weight, preferred_element_type=jnp.float32)  11.6 us
  transfers between devices with their start and end apart: 3, of which 3 were waited for; matrix products, arithmetic and copies ran while one was open for 2% of the time, Pallas kernels for 0%

commit v1 on v0

--- a/solution.py
+++ b/solution.py
@@ -76,7 +76,10 @@
         precision=HIGHEST_PRECISION,
         preferred_element_type=jnp.float32,
     )
-    state_grad, total_grad = lax.psum((local_state_grad, local_total_grad), ("row", "col"))
+    open_members_all = lambda chunk, axis_key, bus_axis: lax.psum(
+        lax.psum(chunk, axis_key), bus_axis
+    )
+    state_grad, total_grad = open_members_all((local_state_grad, local_total_grad), "row", "col")
     grad_relu_query = (
         jnp.einsum(
             "thm,hjm->thj",

time: 549 us -> 531 us (0.967)
  blocking collectives: 123 us -> 86 us
  waiting for transfers between devices: 358 us -> 375 us
    psum x0 -> x2, waiting for transfers between devices: none -> 89.6 us  [the longest x1 45.9 us: body(): lax.psum(lax.psum(chunk, axis_key), bus_axis)]
    psum x1, waiting for transfers between devices: 109 us -> 35.2 us  [body(): key_state, key_total = lax.psum((local_state, local_total), ('row', 'col'))]
    psum x1 -> x2, blocking collectives: 59.9 us -> 23 us  [the longest x1 16.2 us: body(): lax.psum(lax.psum(chunk, axis_key), bus_axis)]
    unnamed x5 -> x7, waiting for transfers between devices: 249 us -> 250 us
  transfers between devices with their start and end apart: 3 -> 5, of which waited for: 3 -> 5; matrix products, arithmetic and copies ran while one was open for 2% -> 4% of each run, Pallas kernels for 0% -> 0%
where the time goes in v1:
time: 531 us
  waiting for transfers between devices  375 us (71%)
  blocking collectives  86 us (16%)
  matrix products  43.2 us (8%)
  between operations  14.7 us (3%)
  local copies, waits for them, and re-layouts  11.3 us (2%)
    unnamed x7, waiting for transfers between devices  250 us
    psum x1, blocking collectives, body(): key_state, key_total = lax.psum((local_state, local_total), ('row', 'col'))  63 us
    psum x1, waiting for transfers between devices, body(): lax.psum(lax.psum(chunk, axis_key), bus_axis)  45.9 us
    psum x1, waiting for transfers between devices, body(): lax.psum(chunk, axis_key)  43.7 us
    psum x1, waiting for transfers between devices, body(): key_state, key_total = lax.psum((local_state, local_total), ('row', 'col'))  35.2 us
    psum x1, blocking collectives, body(): lax.psum(lax.psum(chunk, axis_key), bus_axis)  16.2 us
    dot_general x1, matrix products, body(): lax.dot_general(token_rows, stacked, (((0,), (0,)), ((), ())), preferred_...  12.2 us
    dot_general x3, matrix products, project(): jnp.dot(token_rows, weight, preferred_element_type=jnp.float32)  11.5 us
  transfers between devices with their start and end apart: 5, of which 5 were waited for; matrix products, arithmetic and copies ran while one was open for 4% of the time, Pallas kernels for 0%

profile of v1, /device:TPU:1, one launch (start us, length us, event | category | flops | bytes accessed | tf_op | source)
XLA Modules:
  0.0 530.6 jit_solution(56521412094113392)
XLA Ops:
  8.2 4.7 broadcast_maximum_fusion.1
  13.0 2.1 convolution_convert_fusion
  15.1 1.1 fusion.21
  16.3 4.6 broadcast_compare_fusion.1
  21.2 63.0 %psum.43 = f32[10,112]{1,0:T(8,128)S(1)} all-reduce(f32[10,112]{1,0:T(8,128)S(1)} %reduce_sum.21), channel_id=1, replica_groups=mesh['dp'=4,'row'=4,'col'=8] {'row','col'}, use_global_device_ids=true, to_apply=%region_2.3 | all-reduce | flops 1120 | bytes 8960 | tf_op jit(solution)/shard_map/psum | solution.py:41
  85.5 1.2 fusion.19
  86.8 35.2 %all-reduce.7.cloned.1.call-done = f32[10,112,112]{2,1,0:T(8,128)} async-done(((f32[10,112,112]{2,1,0:T(8,128)}), f32[10,112,112]{2,1,0:T(8,128)}) %all-reduce.7.cloned.1.call-update) | async-done | bytes 501776 | tf_op jit(solution)/shard_map/psum | solution.py:41
  122.0 1.7 fusion.9
  123.7 43.7 %all-reduce.9.cloned.1.call-done = f32[10,112,112]{2,1,0:T(8,128)} async-done(((f32[10,112,112]{2,1,0:T(8,128)}), f32[10,112,112]{2,1,0:T(8,128)}) %all-reduce.9.cloned.1.call-update) | async-done | bytes 501776 | tf_op jit(solution)/shard_map/psum | solution.py:80
  168.0 6.7 %psum.46 = f32[10,112]{1,0:T(8,128)S(1)} all-reduce(f32[10,112]{1,0:T(8,128)S(1)} %bitcast.132), channel_id=1, replica_groups=mesh['dp'=4,'row'=4,'col'=8] {'row'}, use_global_device_ids=true, to_apply=%region_6.7 | all-reduce | flops 1120 | bytes 8960 | tf_op jit(solution)/shard_map/psum | solution.py:80
  174.8 16.2 %psum.47 = f32[10,112]{1,0:T(8,128)S(1)} all-reduce(f32[10,112]{1,0:T(8,128)S(1)} %psum.46), channel_id=1, replica_groups=mesh['dp'=4,'row'=4,'col'=8] {'col'}, use_global_device_ids=true, to_apply=%region_7.8 | all-reduce | flops 1120 | bytes 8960 | tf_op jit(solution)/shard_map/psum | solution.py:79
  191.0 1.6 fusion.8
  192.6 45.9 %all-reduce.11.cloned.1.call-done = f32[10,112,112]{2,1,0:T(8,128)} async-done(((f32[10,112,112]{2,1,0:T(8,128)}), f32[10,112,112]{2,1,0:T(8,128)}) %all-reduce.11.cloned.1.call-update) | async-done | bytes 501776 | tf_op jit(solution)/shard_map/psum | solution.py:79
  238.5 1.7 convolution_convert_fusion.3
  240.2 1.5 fusion.7
  241.8 12.2 %multiply_bitcast_fusion = f32[2240,3360]{0,1:T(8,128)} fusion(bf16[128,3360]{0,1:T(8,128)(2,1)S(1)} %bitcast.110, bf16[1,16,8,2240]{3,2,1,0:T(8,128)(2,1)S(1)} %copy-done), kind=kOutput, calls=%fused_computation | convolution fusion | flops 1934284800 | bytes 31539200 | tf_op jit(solution)/shard_map/dot_general | solution.py:132
  255.9 234.1 %all-reduce.13.cloned.1.call-done = f32[2240,3360]{0,1:T(8,128)} async-done(((f32[2240,3360]{0,1:T(8,128)}), f32[2240,3360]{0,1:T(8,128)}) %all-reduce.13.cloned.1.call-update) | async-done | bytes 30105616
  490.0 3.7 constant_dynamic-slice_fusion
  493.7 4.1 fusion.22
  497.9 4.1 convolution_add_fusion.1
  502.1 1.6 fusion
  503.6 1.1 copy.31
  504.7 15.9 %reduce-scatter.5.cloned.1.call-done = f32[70,840]{0,1:T(8,128)} async-done(((f32[70,3360]{0,1:T(8,128)}), f32[70,840]{0,1:T(8,128)}) %reduce-scatter.5.cloned.1.call-update) | async-done | bytes 235216
  520.6 1.1 fusion.20
  (42 shorter events, 7.1 us)
Async XLA Ops:
  7.2 1.1 copy-start
  7.2 114.8 %all-reduce.7.cloned.1.call-start = ((), (), s32[]{:S(2)}) async-start(), calls=%async_computation.1 | async-start | bytes 1146880 | tf_op jit(solution)/shard_map/psum | solution.py:41
  8.2 4.7 copy-start.2
  15.1 69.0 %copy-start.3 = (bf16[1,16,8,1120]{3,2,1,0:T(8,128)(2,1)S(1)}, bf16[1,16,8,1120]{3,2,1,0:T(8,128)(2,1)}, u32[]{:S(2)}) copy-start(bf16[1,16,8,1120]{3,2,1,0:T(8,128)(2,1)} %param.9) | copy-start | bytes 860164
  16.3 151.1 %all-reduce.9.cloned.1.call-start = ((), (), s32[]{:S(2)}) async-start(), calls=%async_computation.2 | async-start | bytes 1146880 | tf_op jit(solution)/shard_map/psum | solution.py:80
  86.7 151.8 %all-reduce.11.cloned.1.call-start = ((), (), s32[]{:S(2)}) async-start(), calls=%async_computation.3 | async-start | bytes 1146880 | tf_op jit(solution)/shard_map/psum | solution.py:79
  167.4 322.6 %all-reduce.13.cloned.1.call-start = ((), (), s32[]{:S(2)}) async-start(), calls=%async_computation.4 | async-start | bytes 61931520
  254.0 0.7 copy-start.4
  254.1 266.6 %reduce-scatter.5.cloned.1.call-start = ((), (), s32[]{:S(2)}) async-start(), calls=%async_computation.5 | async-start | bytes 2150400
  493.7 8.3 %slice-start = ((s8[5160960]{0:T(1024)(128)(4,1)}), s8[4194304]{0:T(1024)(128)(4,1)S(1)}, s32[]{:S(2)}) async-start(s8[5160960]{0:T(1024)(128)(4,1)} %bitcast.108), calls=%async_computation.6 | async-start | bytes 8388608
  497.9 4.2 slice-start.1
  502.0 22.0 %copy-start.1 = (bf16[1,16,8,2240]{3,2,1,0:T(8,128)(2,1)S(1)}, bf16[1,16,8,2240]{3,2,1,0:T(8,128)(2,1)}, u32[]{:S(2)}) copy-start(bf16[1,16,8,2240]{3,2,1,0:T(8,128)(2,1)} %param.5) | copy-start | bytes 1720324
Sparse Core Ops, SparseCore 0:
  16.4 105.5 all-reduce.6
  124.5 42.8 all-reduce.8
  169.9 68.5 all-reduce.10
  254.2 235.7 all-reduce.12
  493.8 26.7 reduce-scatter.4
